TPU v7x, 256 devices: a whole 4x4x8 slice. The times are simulated.
256 devices in a mesh: scan: 4 (over y), slab: 64 (over z, x, core).
Axes of the slice: x: 4, y: 4, z: 8, core: 2. Of those that a mesh axis runs over, the one named last changes fastest.
Arguments:
- volume: float32 [4, 32768, 1024], P('scan', 'slab'), may hold values from -108 to 108
- velocity0: float32 [4, 32768], P('scan', 'slab'), may hold values from -0.5 to 0.5
- fetch_slab: int32 [4, 2, 32768, 1], P('scan', None, 'slab'), may hold values from 0 to 63; in each aligned block of 512 rows (0 to 511, 512 to 1023, ..., all dimensions but the last counted through in order) at most 12 rows name the same one
- fetch_row: int32 [4, 2, 32768], P('scan', None, 'slab'), may hold values from 0 to 511
- modulus_class: int32 [4, 32768], P('scan', 'slab'), may hold values from 0 to 3
- modulus_table: float32 [4], replicated, may hold values from 200 to 3000
Outputs:
- velocity: float32 [4, 32768], P('scan', 'slab')
- misfit: float32 [4, 32768, 1024], P('scan', 'slab')
Inputs may be any that keep to these rules, and one draw needn't show every extreme that they name: `fetch_slab`: among the rows of one device for one direction, at most 12 name the same slab, a bound that some block reaches of them.
All inputs are finite; a program needn't handle non-finite values.
Results may differ from a plain program's by a relative error of at most 0.00011.
Values sent between devices are 32-bit elements; how exact they have to be, the bound alone decides.
A program may use at most 64 MiB of HBM per device.

v0:
```python
import math
import jax
import jax.numpy as jnp
from jax import lax
from jax.sharding import PartitionSpec as P

Y = 1024
BAND = 32
ITERS = 2
root_three = math.sqrt(3.0)
pole_value = math.sqrt(3.0) - 2.0


def with_halo(cells, sides, width):
    for axis, dim in sides:
        count = lax.axis_size(axis)
        ends = count - 1
        head = lax.slice_in_dim(cells, 0, width, axis=dim)
        tail = lax.slice_in_dim(cells, cells.shape[dim] - width, cells.shape[dim], axis=dim)
        cells = jnp.concatenate(
            [
                lax.ppermute(tail, axis, [(i, (i + 1) % count) for i in range(ends)]),
                cells,
                lax.ppermute(head, axis, [((i + 1) % count, i) for i in range(ends)]),
            ],
            axis=dim,
        )
    return cells


def passed_along(block, axis, distance):
    devices = range(lax.axis_size(axis))
    route = [(i - distance, i) for i in devices if i - distance in devices]
    return lax.ppermute(block, axis, route)


def filter_block(block_width, band_reach):
    offsets = (
        lax.broadcasted_iota(jnp.int32, (3 * block_width, block_width), 0)
        - block_width
        - lax.broadcasted_iota(jnp.int32, (3 * block_width, block_width), 1)
    )
    distance = jnp.abs(offsets)
    parity = 1.0 - 2.0 * (distance % 2).astype(jnp.float32)
    magnitude = jnp.exp(distance.astype(jnp.float32) * math.log(-pole_value))
    return jnp.where(
        distance <= band_reach, root_three * parity * magnitude, jnp.zeros_like(magnitude)
    )


def prefilter(voxels):
    length = voxels.shape[1]
    block_width = min(128, length)
    matrix = filter_block(block_width, BAND)
    padded = jnp.pad(voxels, ((0, 0), (block_width, block_width)))
    pieces = []
    for number in range(length // block_width):
        window = padded[:, number * block_width : number * block_width + 3 * block_width]
        pieces.append(
            jnp.dot(
                window, matrix, preferred_element_type=jnp.float32, precision=lax.Precision.HIGHEST
            )
        )
    return jnp.concatenate(pieces, axis=1)


def taylor_terms(coeffs):
    padded = jnp.pad(coeffs, ((0, 0), (1, 1)))
    before = padded[:, :-2]
    after = padded[:, 2:]
    value = (before + 4.0 * coeffs + after) / 6.0
    slope = 0.5 * (after - before)
    bend = after - 2.0 * coeffs + before
    return (value, slope, bend)


def residuals(forward, backward, voxels, velocity):
    moved = velocity[:, None]
    fwd_value, fwd_slope, fwd_bend = taylor_terms(forward)
    bwd_value, bwd_slope, bwd_bend = taylor_terms(backward)
    res_fwd = fwd_value + moved * fwd_slope + 0.5 * moved * moved * fwd_bend - voxels
    jac_fwd = fwd_slope + moved * fwd_bend
    res_bwd = bwd_value - moved * bwd_slope + 0.5 * moved * moved * bwd_bend - voxels
    jac_bwd = moved * bwd_bend - bwd_slope
    return (res_fwd, jac_fwd, res_bwd, jac_bwd)


def row_terms(forward, backward, voxels, velocity):
    res_fwd, jac_fwd, res_bwd, jac_bwd = residuals(forward, backward, voxels, velocity)
    linear = jnp.sum(jac_fwd * res_fwd + jac_bwd * res_bwd, axis=1)
    curvature = jnp.sum(jac_fwd * jac_fwd + jac_bwd * jac_bwd, axis=1)
    return (linear, curvature)


def plane_stencil(field):
    count_rows = field.shape[0]
    hops = Y // count_rows
    rimmed = with_halo(field[None, :], (("slab", 1),), 1)[0]
    lower = passed_along(field, "slab", hops)
    upper = passed_along(field, "slab", -hops)
    return 4.0 * field - rimmed[:-2] - rimmed[2:] - lower - upper


def on_device(volume, velocity0, fetch_slab, fetch_row, modulus_class, modulus_table):
    own_scan = volume[0]
    count_rows = own_scan.shape[0]
    devices = lax.axis_size("slab")
    capacity = max(2, 3 * count_rows // (2 * devices))
    ahead_rows = passed_along(own_scan, "scan", -1)
    behind = passed_along(own_scan, "scan", 1)
    peer_ids = fetch_slab[0, :, :, 0]
    wanted_rows = fetch_row[0]
    one_hot = (peer_ids[:, :, None] == lax.broadcasted_iota(jnp.int32, (1, 1, devices), 2)).astype(
        jnp.int32
    )
    running = jnp.cumsum(one_hot, axis=1) - one_hot
    slot_ids = jnp.sum(running * one_hot, axis=2)
    direction_ids = lax.broadcasted_iota(jnp.int32, (2, count_rows), 0)
    request_table = (
        jnp.zeros((2, devices, capacity), jnp.int32)
        .at[direction_ids, peer_ids, slot_ids]
        .set(wanted_rows)
    )
    asked_rows = lax.all_to_all(request_table, "slab", split_axis=1, concat_axis=1, tiled=True)
    forward_rows = jnp.take(ahead_rows, asked_rows[0], axis=0)
    backward_rows = jnp.take(behind, asked_rows[1], axis=0)
    arrived = lax.all_to_all(
        jnp.stack([forward_rows, backward_rows]), "slab", split_axis=1, concat_axis=1, tiled=True
    )
    fetched = arrived[direction_ids, peer_ids, slot_ids]
    filtered = prefilter(fetched.reshape(2 * count_rows, fetched.shape[2]))
    forward = filtered[:count_rows]
    backward = filtered[count_rows:]
    classes = lax.broadcasted_iota(jnp.int32, (1, modulus_table.shape[0]), 1)
    weight = jnp.sum(
        jnp.where(
            modulus_class[0][:, None] == classes,
            modulus_table[None, :],
            jnp.zeros_like(modulus_table)[None, :],
        ),
        axis=1,
    )
    stiffness = jnp.sqrt(weight)
    velocity = velocity0[0]
    for iteration in range(ITERS):
        linear, curvature = row_terms(forward, backward, own_scan, velocity)
        gradient = linear + stiffness * plane_stencil(stiffness * velocity)
        diagonal = curvature + 4.0 * stiffness * stiffness
        direction = gradient / diagonal
        scaled_dir = stiffness * direction
        bend_term = scaled_dir * plane_stencil(scaled_dir)
        totals = lax.psum(
            (jnp.sum(direction * gradient), jnp.sum(curvature * direction * direction + bend_term)),
            ("scan", "slab"),
        )
        velocity = velocity - totals[0] / totals[1] * direction
    res_fwd, jac_fwd, res_bwd, jac_bwd = residuals(forward, backward, own_scan, velocity)
    return (velocity[None, :], (res_fwd + res_bwd)[None])


def solution(mesh):
    return jax.shard_map(
        on_device,
        mesh=mesh,
        in_specs=(
            P("scan", "slab", None),
            P("scan", "slab"),
            P("scan", None, "slab", None),
            P("scan", None, "slab"),
            P("scan", "slab"),
            P(),
        ),
        out_specs=(P("scan", "slab"), P("scan", "slab", None)),
        check_vma=False,
    )
```

profile of v0, /device:TPU:1, one launch (start us, length us, event | category | flops | bytes accessed | tf_op | source)
XLA Modules:
  0.0 537.1 jit_solution(10035754950157322251)
XLA Ops:
  0.7 2.9 copy.63
  4.9 6.0 %collective-permute-start.1 = (f32[512,1024]{0,1:T(8,128)}, f32[512,1024]{0,1:T(8,128)}, u32[]{:S(2)}, u32[]{:S(2)}) collective-permute-start(f32[512,1024]{0,1:T(8,128)} %bitcast.6), channel_id=1, source_target_pairs={{0,64},{64,128},{128,192},{1,65},{65,129},{129,193},{2,66},{66,130... | collective-permute-start | bytes 6291464 | tf_op jit(solution)/shard_map/ppermute | solution.py:34
  14.2 4.3 scatter_custom_fusion
  18.7 23.1 %all_to_all.10 = s32[2,64,12]{2,0,1:T(2,128)S(1)} all-to-all(s32[2,64,12]{2,0,1:T(2,128)S(1)} %copy.60), channel_id=1, replica_groups=mesh['scan'=4,'slab'=64] {'slab'}, dimensions={1} | all-to-all | bytes 12288 | tf_op jit(solution)/shard_map/all_to_all | solution.py:124
  42.7 8.4 %collective-permute-done = f32[512,1024]{0,1:T(8,128)} collective-permute-done((f32[512,1024]{0,1:T(8,128)}, f32[512,1024]{0,1:T(8,128)}, u32[]{:S(2)}, u32[]{:S(2)}) %collective-permute-start) | collective-permute-done | bytes 2097184 | tf_op jit(solution)/shard_map/ppermute | solution.py:34
  53.0 3.6 gather_fusion.1
  56.6 4.6 reshape.161
  63.1 3.7 gather_fusion.2
  66.8 4.6 reshape.165
  71.4 3.8 select_bitcast_fusion
  75.3 4.2 pad_maximum_fusion
  79.5 12.0 %copy.70 = f32[2,64,12,1024]{3,0,2,1:T(2,128)} copy(f32[2,64,12,1024]{3,2,1,0:T(8,128)} %pad_maximum_fusion) | data formatting | bytes 12582912 | tf_op jit(solution)/shard_map/stack | solution.py:128
  91.4 15.3 %all-to-all-start.1 = ((f32[2,64,12,1024]{3,0,2,1:T(2,128)}), f32[2,64,12,1024]{3,0,2,1:T(2,128)}, u32[]{:S(2)}, u32[]{:S(2)}) async-start(f32[2,64,12,1024]{3,0,2,1:T(2,128)} %copy.70), calls=%async_computation.1 | async-start | bytes 12582912 | tf_op jit(solution)/shard_map/all_to_all | solution.py:127
  106.9 3.3 collective-permute-start.4
  112.0 4.8 collective-permute-start.2
  116.9 13.8 %collective-permute-start.3 = (f32[1,1]{1,0:T(1,128)}, f32[1,1]{1,0:T(1,128)}, u32[]{:S(2)}, u32[]{:S(2)}) collective-permute-start(f32[1,1]{1,0:T(1,128)} %get-tuple-element.67), channel_id=1, source_target_pairs={{1,0},{2,1},{3,2},{4,3},{5,4},{6,5},{7,6},{8,7},{9,8},{10,9},{11,1... | collective-permute-start | bytes 20 | tf_op jit(solution)/shard_map/ppermute | solution.py:24
  132.1 113.6 %all-to-all-done.1 = f32[2,64,12,1024]{3,0,2,1:T(2,128)} async-done(((f32[2,64,12,1024]{3,0,2,1:T(2,128)}), f32[2,64,12,1024]{3,0,2,1:T(2,128)}, u32[]{:S(2)}, u32[]{:S(2)}) %all-to-all-start.1) | async-done | bytes 6291488 | tf_op jit(solution)/shard_map/all_to_all | solution.py:127
  245.6 9.1 %copy.71 = f32[2,64,12,1024]{3,1,2,0:T(8,128)} copy(f32[2,64,12,1024]{3,0,2,1:T(2,128)} %all-to-all-done.1) | data formatting | bytes 12582912 | tf_op jit(solution)/shard_map/all_to_all | solution.py:127
  254.7 21.5 %gather_fusion = f32[1024,1024]{1,0:T(8,128)} fusion(f32[2,64,12,1024]{3,1,2,0:T(8,128)} %copy.71, s32[1024]{0:T(1024)S(1)} %bitcast.67), kind=kCustom, calls=%fused_computation.2 | custom fusion | bytes 8400896 | tf_op jit(solution)/shard_map/gather | solution.py:130
  276.2 3.3 fusion.35
  293.9 7.1 %add_reduce_fusion.2 = (f32[512]{0:T(512)S(1)}, f32[512]{0:T(512)S(1)}, f32[512,1024]{0,1:T(8,128)S(1)}, f32[512,1024]{0,1:T(8,128)}, f32[512,1024]{0,1:T(8,128)...) fusion(f32[512]{0:T(512)S(1)} %bitcast.69, f32[1,512,1024]{1,2,0:T(8,128)} %copy.63, ...), kind=kLoop, calls=%fused_computation.14 | loop fusion | flops 20970496 | bytes 18884608 | tf_op jit(solution)/shard_map/reduce_sum | solution.py:91
  301.0 3.1 collective-permute-start.8
  306.0 7.2 %collective-permute-start.6 = (f32[1,1]{1,0:T(1,128)}, f32[1,1]{1,0:T(1,128)}, u32[]{:S(2)}, u32[]{:S(2)}) collective-permute-start(f32[1,1]{1,0:T(1,128)} %get-tuple-element.62), channel_id=1, source_target_pairs={{0,1},{1,2},{2,3},{3,4},{4,5},{5,6},{6,7},{7,8},{8,9},{9,10},{10,1... | collective-permute-start | bytes 20 | tf_op jit(solution)/shard_map/ppermute | solution.py:22
  315.2 3.3 collective-permute-done.7
  320.5 78.0 %all-reduce.4 = (f32[]{:T(128)}, f32[]{:T(128)}) all-reduce(f32[]{:T(128)} %get-tuple-element.22, f32[]{:T(128)} %get-tuple-element.21), channel_id=1, replica_groups=mesh['scan'=4,'slab'=64] {'scan','slab'}, use_global_device_ids=true, to_apply=%region_8.10 | all-reduce | flops 2 | bytes 16 | tf_op jit(solution)/shard_map/psum | solution.py:152
  404.3 5.1 collective-permute-start.10
  411.4 5.5 %add_reduce_fusion = (f32[512]{0:T(512)S(1)}, f32[512]{0:T(512)S(1)}) fusion(f32[512,1024]{0,1:T(8,128)} %get-tuple-element.42, f32[512,1024]{0,1:T(8,128)} %get-tuple-element.41, f32[512,1024]{0,1:T(8,128)} %get-tuple-element.40, f32[512,1024]{0,1:T(8,128)} %get-tuple-element.39, f32[512]{0:T(512)S(1)} %get-tuple-element.33, ...), kind=kLoop, calls=%fused_computation.10 | loop fusion | flops 12581888 | bytes 14690304 | tf_op jit(solution)/shard_map/reduce_sum | solution.py:91
  422.4 5.9 %collective-permute-start.14 = (f32[1,1]{1,0:T(1,128)}, f32[1,1]{1,0:T(1,128)}, u32[]{:S(2)}, u32[]{:S(2)}) collective-permute-start(f32[1,1]{1,0:T(1,128)} %get-tuple-element.52), channel_id=1, source_target_pairs={{0,1},{1,2},{2,3},{3,4},{4,5},{5,6},{6,7},{7,8},{8,9},{9,10},{10,1... | collective-permute-start | bytes 20 | tf_op jit(solution)/shard_map/ppermute | solution.py:22
  430.3 3.3 collective-permute-done.15
  435.6 89.2 %all-reduce.3 = (f32[]{:T(128)}, f32[]{:T(128)}) all-reduce(f32[]{:T(128)} %get-tuple-element.20, f32[]{:T(128)} %get-tuple-element.19), channel_id=1, replica_groups=mesh['scan'=4,'slab'=64] {'scan','slab'}, use_global_device_ids=true, to_apply=%region_14.16 | all-reduce | flops 2 | bytes 16 | tf_op jit(solution)/shard_map/psum | solution.py:152
  526.1 7.8 %add_bitcast_fusion = f32[1,512,1024]{1,2,0:T(8,128)} fusion(f32[512,1024]{0,1:T(8,128)} %get-tuple-element.41, f32[512,1024]{0,1:T(8,128)} %get-tuple-element.38, f32[512,1024]{0,1:T(8,128)} %get-tuple-element.42, f32[512,1024]{0,1:T(8,128)} %get-tuple-element.40, f32[512,1024]{0,1:T(8,128)S(1)} %get-tuple-element.37, f32[512,1024]{0,1:T(8,128)} %get-tuple-element.39, ...), kind=kLoop, calls=%fused_computation.9 | loop fusion | flops 5767168 | bytes 16781312 | tf_op jit(solution)/shard_map/broadcast_in_dim | solution.py:158
  534.0 2.9 copy.72
  (104 shorter events, 48.7 us)
Async XLA Ops:
  0.6 13.3 %copy-start.7 = (s32[3]{0:T(128)S(1)}, s32[3]{0:T(128)}, u32[]{:S(2)}) copy-start(s32[3]{0:T(128)} %constant.79) | copy-start | bytes 40
  0.6 13.4 %copy-start.8 = (s32[3]{0:T(128)S(1)}, s32[3]{0:T(128)}, u32[]{:S(2)}) copy-start(s32[3]{0:T(128)} %constant.82) | copy-start | bytes 40
  0.7 10.2 %copy-start.2 = (s32[1,2,512,1]{2,3,1,0:T(1,128)S(1)}, s32[1,2,512,1]{2,3,1,0:T(1,128)}, u32[]{:S(2)}) copy-start(s32[1,2,512,1]{2,3,1,0:T(1,128)} %param.10) | copy-start | bytes 12292
  0.7 13.5 %copy-start.4 = (s32[1,2,512]{2,1,0:T(2,128)S(1)}, s32[1,2,512]{2,1,0:T(2,128)}, u32[]{:S(2)}) copy-start(s32[1,2,512]{2,1,0:T(2,128)} %param.11) | copy-start | bytes 12292
  3.6 47.5 %collective-permute-start = (f32[512,1024]{0,1:T(8,128)}, f32[512,1024]{0,1:T(8,128)}, u32[]{:S(2)}, u32[]{:S(2)}) collective-permute-start(f32[512,1024]{0,1:T(8,128)} %bitcast.6), channel_id=1, source_target_pairs={{64,0},{128,64},{192,128},{65,1},{129,65},{193,129},{66,2},{130,66... | collective-permute-start | bytes 6291464 | tf_op jit(solution)/shard_map/ppermute | solution.py:34
  4.9 56.4 %collective-permute-start.1 = (f32[512,1024]{0,1:T(8,128)}, f32[512,1024]{0,1:T(8,128)}, u32[]{:S(2)}, u32[]{:S(2)}) collective-permute-start(f32[512,1024]{0,1:T(8,128)} %bitcast.6), channel_id=1, source_target_pairs={{0,64},{64,128},{128,192},{1,65},{65,129},{129,193},{2,66},{66,130... | collective-permute-start | bytes 6291464 | tf_op jit(solution)/shard_map/ppermute | solution.py:34
  91.4 15.3 %copy-start.5 = (s32[1,512]{1,0:T(1,128)S(1)}, s32[1,512]{1,0:T(1,128)}, u32[]{:S(2)}) copy-start(s32[1,512]{1,0:T(1,128)} %param.12) | copy-start | bytes 6148
  91.4 15.4 %copy-start.6 = (f32[4]{0:T(128)S(1)}, f32[4]{0:T(128)}, u32[]{:S(2)}) copy-start(f32[4]{0:T(128)} %param.13) | copy-start | bytes 52
  91.4 15.4 %copy-start.1 = (f32[1,512]{1,0:T(1,128)S(1)}, f32[1,512]{1,0:T(1,128)}, u32[]{:S(2)}) copy-start(f32[1,512]{1,0:T(1,128)} %param.9) | copy-start | bytes 6148
  91.4 154.2 %all-to-all-start.1 = ((f32[2,64,12,1024]{3,0,2,1:T(2,128)}), f32[2,64,12,1024]{3,0,2,1:T(2,128)}, u32[]{:S(2)}, u32[]{:S(2)}) async-start(f32[2,64,12,1024]{3,0,2,1:T(2,128)} %copy.70), calls=%async_computation.1 | async-start | bytes 12582912 | tf_op jit(solution)/shard_map/all_to_all | solution.py:127
  106.9 194.1 %collective-permute-start.4 = (f32[512]{0:T(512)S(1)}, f32[512]{0:T(512)S(1)}, u32[]{:S(2)}, u32[]{:S(2)}) collective-permute-start(f32[512]{0:T(512)S(1)} %get-tuple-element.69), channel_id=1, source_target_pairs={{0,2},{1,3},{2,4},{3,5},{4,6},{5,7},{6,8},{7,9},{8,10},{9,11},{10,... | collective-permute-start | bytes 6152 | tf_op jit(solution)/shard_map/ppermute | solution.py:34
  110.1 190.8 %collective-permute-start.5 = (f32[512]{0:T(512)S(1)}, f32[512]{0:T(512)S(1)}, u32[]{:S(2)}, u32[]{:S(2)}) collective-permute-start(f32[512]{0:T(512)S(1)} %get-tuple-element.69), channel_id=1, source_target_pairs={{2,0},{3,1},{4,2},{5,3},{6,4},{7,5},{8,6},{9,7},{10,8},{11,9},{12,... | collective-permute-start | bytes 6152 | tf_op jit(solution)/shard_map/ppermute | solution.py:34
  112.0 18.7 %collective-permute-start.2 = (f32[1,1]{1,0:T(1,128)}, f32[1,1]{1,0:T(1,128)}, u32[]{:S(2)}, u32[]{:S(2)}) collective-permute-start(f32[1,1]{1,0:T(1,128)} %get-tuple-element.66), channel_id=1, source_target_pairs={{0,1},{1,2},{2,3},{3,4},{4,5},{5,6},{6,7},{7,8},{8,9},{9,10},{10,1... | collective-permute-start | bytes 20 | tf_op jit(solution)/shard_map/ppermute | solution.py:22
  116.9 13.9 %collective-permute-start.3 = (f32[1,1]{1,0:T(1,128)}, f32[1,1]{1,0:T(1,128)}, u32[]{:S(2)}, u32[]{:S(2)}) collective-permute-start(f32[1,1]{1,0:T(1,128)} %get-tuple-element.67), channel_id=1, source_target_pairs={{1,0},{2,1},{3,2},{4,3},{5,4},{6,5},{7,6},{8,7},{9,8},{10,9},{11,1... | collective-permute-start | bytes 20 | tf_op jit(solution)/shard_map/ppermute | solution.py:24
  276.2 3.3 copy-start
  301.0 18.8 %collective-permute-start.8 = (f32[512]{0:T(512)S(1)}, f32[512]{0:T(512)S(1)}, u32[]{:S(2)}, u32[]{:S(2)}) collective-permute-start(f32[512]{0:T(512)S(1)} %get-tuple-element.34), channel_id=1, source_target_pairs={{0,2},{1,3},{2,4},{3,5},{4,6},{5,7},{6,8},{7,9},{8,10},{9,11},{10,... | collective-permute-start | bytes 6152 | tf_op jit(solution)/shard_map/ppermute | solution.py:34
  304.1 15.7 %collective-permute-start.9 = (f32[512]{0:T(512)S(1)}, f32[512]{0:T(512)S(1)}, u32[]{:S(2)}, u32[]{:S(2)}) collective-permute-start(f32[512]{0:T(512)S(1)} %get-tuple-element.34), channel_id=1, source_target_pairs={{2,0},{3,1},{4,2},{5,3},{6,4},{7,5},{8,6},{9,7},{10,8},{11,9},{12,... | collective-permute-start | bytes 6152 | tf_op jit(solution)/shard_map/ppermute | solution.py:34
  306.0 9.2 %collective-permute-start.6 = (f32[1,1]{1,0:T(1,128)}, f32[1,1]{1,0:T(1,128)}, u32[]{:S(2)}, u32[]{:S(2)}) collective-permute-start(f32[1,1]{1,0:T(1,128)} %get-tuple-element.62), channel_id=1, source_target_pairs={{0,1},{1,2},{2,3},{3,4},{4,5},{5,6},{6,7},{7,8},{8,9},{9,10},{10,1... | collective-permute-start | bytes 20 | tf_op jit(solution)/shard_map/ppermute | solution.py:22
  313.3 5.2 collective-permute-start.7
  399.8 18.5 %collective-permute-start.12 = (f32[512]{0:T(512)S(1)}, f32[512]{0:T(512)S(1)}, u32[]{:S(2)}, u32[]{:S(2)}) collective-permute-start(f32[512]{0:T(512)S(1)} %get-tuple-element.32), channel_id=1, source_target_pairs={{0,2},{1,3},{2,4},{3,5},{4,6},{5,7},{6,8},{7,9},{8,10},{9,11},{10,... | collective-permute-start | bytes 6152 | tf_op jit(solution)/shard_map/ppermute | solution.py:34
  402.4 15.8 %collective-permute-start.13 = (f32[512]{0:T(512)S(1)}, f32[512]{0:T(512)S(1)}, u32[]{:S(2)}, u32[]{:S(2)}) collective-permute-start(f32[512]{0:T(512)S(1)} %get-tuple-element.32), channel_id=1, source_target_pairs={{2,0},{3,1},{4,2},{5,3},{6,4},{7,5},{8,6},{9,7},{10,8},{11,9},{12,... | collective-permute-start | bytes 6152 | tf_op jit(solution)/shard_map/ppermute | solution.py:34
  404.3 12.6 %collective-permute-start.10 = (f32[1,1]{1,0:T(1,128)}, f32[1,1]{1,0:T(1,128)}, u32[]{:S(2)}, u32[]{:S(2)}) collective-permute-start(f32[1,1]{1,0:T(1,128)} %get-tuple-element.56), channel_id=1, source_target_pairs={{0,1},{1,2},{2,3},{3,4},{4,5},{5,6},{6,7},{7,8},{8,9},{9,10},{10,1... | collective-permute-start | bytes 20 | tf_op jit(solution)/shard_map/ppermute | solution.py:22
  409.4 7.5 %collective-permute-start.11 = (f32[1,1]{1,0:T(1,128)}, f32[1,1]{1,0:T(1,128)}, u32[]{:S(2)}, u32[]{:S(2)}) collective-permute-start(f32[1,1]{1,0:T(1,128)} %get-tuple-element.57), channel_id=1, source_target_pairs={{1,0},{2,1},{3,2},{4,3},{5,4},{6,5},{7,6},{8,7},{9,8},{10,9},{11,1... | collective-permute-start | bytes 20 | tf_op jit(solution)/shard_map/ppermute | solution.py:24
  418.3 16.6 %collective-permute-start.16 = (f32[512]{0:T(512)S(1)}, f32[512]{0:T(512)S(1)}, u32[]{:S(2)}, u32[]{:S(2)}) collective-permute-start(f32[512]{0:T(512)S(1)} %get-tuple-element.29), channel_id=1, source_target_pairs={{0,2},{1,3},{2,4},{3,5},{4,6},{5,7},{6,8},{7,9},{8,10},{9,11},{10,... | collective-permute-start | bytes 6152 | tf_op jit(solution)/shard_map/ppermute | solution.py:34
  420.6 14.4 %collective-permute-start.17 = (f32[512]{0:T(512)S(1)}, f32[512]{0:T(512)S(1)}, u32[]{:S(2)}, u32[]{:S(2)}) collective-permute-start(f32[512]{0:T(512)S(1)} %get-tuple-element.29), channel_id=1, source_target_pairs={{2,0},{3,1},{4,2},{5,3},{6,4},{7,5},{8,6},{9,7},{10,8},{11,9},{12,... | collective-permute-start | bytes 6152 | tf_op jit(solution)/shard_map/ppermute | solution.py:34
  422.4 7.9 %collective-permute-start.14 = (f32[1,1]{1,0:T(1,128)}, f32[1,1]{1,0:T(1,128)}, u32[]{:S(2)}, u32[]{:S(2)}) collective-permute-start(f32[1,1]{1,0:T(1,128)} %get-tuple-element.52), channel_id=1, source_target_pairs={{0,1},{1,2},{2,3},{3,4},{4,5},{5,6},{6,7},{7,8},{8,9},{9,10},{10,1... | collective-permute-start | bytes 20 | tf_op jit(solution)/shard_map/ppermute | solution.py:22
  428.4 5.2 collective-permute-start.15
  526.1 7.9 %copy-start.3 = (f32[512]{0:T(512)}, f32[512]{0:T(512)S(1)}, u32[]{:S(2)}) copy-start(f32[512]{0:T(512)S(1)} %get-tuple-element.28) | copy-start | bytes 6148
where the time goes:
time: 542 us; the launch traced here: 537 us
  blocking collectives  190 us (35%)
  waiting for transfers between devices  128 us (24%)
  starting transfers between devices  81.8 us (15%)
  local copies, waits for them, and re-layouts  77.3 us (14%)
  other arithmetic  38.1 us (7%)
  matrix products  17 us (3%)
    psum x2, blocking collectives, on_device(): lax.psum((jnp.sum(direction * gradient), jnp.sum(curvature * direction *...  167 us
    all_to_all x1, waiting for transfers between devices, on_device(): lax.all_to_all(jnp.stack([forward_rows, backward_rows]), 'slab', split_ax...  114 us
    ppermute x10, starting transfers between devices, passed_along(): return lax.ppermute(block, axis, route)  23.8 us
    all_to_all x1, blocking collectives, on_device(): lax.all_to_all(request_table, 'slab', split_axis=1, concat_axis=1, tiled=...  23.1 us
    ppermute x4, starting transfers between devices, with_halo(): lax.ppermute(tail, axis, [(i, (i + 1) % count) for i in range(ends)])  23.1 us
    gather x1, local copies, waits for them, and re-layouts, on_device(): fetched = arrived[direction_ids, peer_ids, slot_ids]  21.5 us
    ppermute x4, starting transfers between devices, with_halo(): lax.ppermute(head, axis, [((i + 1) % count, i) for i in range(ends)])  19.6 us
    dot_general x8, matrix products, prefilter(): jnp.dot(window, matrix, preferred_element_type=jnp.float32, precision=lax...  17 us
  transfers between devices with their start and end apart: 19, of which 4 were waited for; matrix products, arithmetic and copies ran while one was open for 16% of the time, Pallas kernels for 0%

commit v1 on v0

--- a/solution.py
+++ b/solution.py
@@ -121,7 +121,11 @@
         .at[direction_ids, peer_ids, slot_ids]
         .set(wanted_rows)
     )
-    asked_rows = lax.all_to_all(request_table, "slab", split_axis=1, concat_axis=1, tiled=True)
+    z = lax.axis_size("slab")
+    r2 = jnp.split(request_table, z, 1)
+    u_next = jnp.stack(r2, 0)
+    parts_out = lax.all_to_all(u_next, "slab", 0, 0)
+    asked_rows = jnp.concatenate(parts_out, 1)
     forward_rows = jnp.take(ahead_rows, asked_rows[0], axis=0)
     backward_rows = jnp.take(behind, asked_rows[1], axis=0)
     arrived = lax.all_to_all(

time: 542 us -> 543 us (level)
  local copies, waits for them, and re-layouts: 77.3 us -> 84.7 us
  waiting for transfers between devices: 128 us -> 121 us
    ppermute x10, waiting for transfers between devices: 8.4 us -> 0.65 us  [passed_along(): return lax.ppermute(block, axis, route)]
    split x0 -> x68, local copies, waits for them, and re-layouts: none -> 7.23 us  [on_device(): r2 = jnp.split(request_table, z, 1)]
  transfers between devices with their start and end apart: 19 -> 19, of which waited for: 4 -> 4; matrix products, arithmetic and copies ran while one was open for 16% -> 18% of each run, Pallas kernels for 0% -> 0%
where the time goes in v1:
time: 543 us; the launch traced here: 537 us
  blocking collectives  190 us (35%)
  waiting for transfers between devices  121 us (22%)
  local copies, waits for them, and re-layouts  84.7 us (16%)
  starting transfers between devices  81.6 us (15%)
  other arithmetic  38.1 us (7%)
  matrix products  17 us (3%)
    psum x2, blocking collectives, on_device(): lax.psum((jnp.sum(direction * gradient), jnp.sum(curvature * direction *...  167 us
    all_to_all x1, waiting for transfers between devices, on_device(): lax.all_to_all(jnp.stack([forward_rows, backward_rows]), 'slab', split_ax...  114 us
    ppermute x10, starting transfers between devices, passed_along(): return lax.ppermute(block, axis, route)  23.7 us
    all_to_all x1, blocking collectives, on_device(): parts_out = lax.all_to_all(u_next, 'slab', 0, 0)  23.1 us
    ppermute x4, starting transfers between devices, with_halo(): lax.ppermute(tail, axis, [(i, (i + 1) % count) for i in range(ends)])  23.1 us
    gather x1, local copies, waits for them, and re-layouts, on_device(): fetched = arrived[direction_ids, peer_ids, slot_ids]  21.5 us
    ppermute x4, starting transfers between devices, with_halo(): lax.ppermute(head, axis, [((i + 1) % count, i) for i in range(ends)])  19.6 us
    dot_general x8, matrix products, prefilter(): jnp.dot(window, matrix, preferred_element_type=jnp.float32, precision=lax...  17 us
  transfers between devices with their start and end apart: 19, of which 4 were waited for; matrix products, arithmetic and copies ran while one was open for 18% of the time, Pallas kernels for 0%

profile of v1, /device:TPU:1, one launch (start us, length us, event | category | flops | bytes accessed | tf_op | source)
XLA Modules:
  0.0 536.8 jit_solution(12122132153639234763)
XLA Ops:
  0.7 2.9 copy.713
  4.9 6.0 %collective-permute-start.1 = (f32[512,1024]{0,1:T(8,128)}, f32[512,1024]{0,1:T(8,128)}, u32[]{:S(2)}, u32[]{:S(2)}) collective-permute-start(f32[512,1024]{0,1:T(8,128)} %bitcast.71), channel_id=1, source_target_pairs={{0,64},{64,128},{128,192},{1,65},{65,129},{129,193},{2,66},{66,130... | collective-permute-start | bytes 6291464 | tf_op jit(solution)/shard_map/ppermute | solution.py:34
  14.2 4.3 scatter_custom_fusion
  26.6 23.1 %all_to_all.10 = s32[64,2,1,12]{3,1,2,0:T(2,128)S(1)} all-to-all(s32[64,2,1,12]{3,1,2,0:T(2,128)S(1)} %constant_dynamic-update-slice_fusion), channel_id=1, replica_groups=mesh['scan'=4,'slab'=64] {'slab'}, dimensions={0} | all-to-all | bytes 12288 | tf_op jit(solution)/shard_map/all_to_all | solution.py:127
  53.0 3.6 gather_fusion.1
  56.6 4.6 reshape.170
  63.1 3.7 gather_fusion.2
  66.8 4.6 reshape.174
  71.4 3.8 select_bitcast_fusion
  75.3 4.2 pad_maximum_fusion
  79.4 12.0 %copy.719 = f32[2,64,12,1024]{3,0,2,1:T(2,128)} copy(f32[2,64,12,1024]{3,2,1,0:T(8,128)} %pad_maximum_fusion) | data formatting | bytes 12582912 | tf_op jit(solution)/shard_map/stack | solution.py:132
  91.4 15.3 %all-to-all-start.1 = ((f32[2,64,12,1024]{3,0,2,1:T(2,128)}), f32[2,64,12,1024]{3,0,2,1:T(2,128)}, u32[]{:S(2)}, u32[]{:S(2)}) async-start(f32[2,64,12,1024]{3,0,2,1:T(2,128)} %copy.719), calls=%async_computation.1 | async-start | bytes 12582912 | tf_op jit(solution)/shard_map/all_to_all | solution.py:131
  106.9 3.3 collective-permute-start.4
  112.0 4.8 collective-permute-start.2
  116.9 13.8 %collective-permute-start.3 = (f32[1,1]{1,0:T(1,128)}, f32[1,1]{1,0:T(1,128)}, u32[]{:S(2)}, u32[]{:S(2)}) collective-permute-start(f32[1,1]{1,0:T(1,128)} %get-tuple-element.135), channel_id=1, source_target_pairs={{1,0},{2,1},{3,2},{4,3},{5,4},{6,5},{7,6},{8,7},{9,8},{10,9},{11,1... | collective-permute-start | bytes 20 | tf_op jit(solution)/shard_map/ppermute | solution.py:24
  132.0 113.6 %all-to-all-done.1 = f32[2,64,12,1024]{3,0,2,1:T(2,128)} async-done(((f32[2,64,12,1024]{3,0,2,1:T(2,128)}), f32[2,64,12,1024]{3,0,2,1:T(2,128)}, u32[]{:S(2)}, u32[]{:S(2)}) %all-to-all-start.1) | async-done | bytes 6291488 | tf_op jit(solution)/shard_map/all_to_all | solution.py:131
  245.6 9.1 %copy.720 = f32[2,64,12,1024]{3,1,2,0:T(8,128)} copy(f32[2,64,12,1024]{3,0,2,1:T(2,128)} %all-to-all-done.1) | data formatting | bytes 12582912 | tf_op jit(solution)/shard_map/all_to_all | solution.py:131
  254.7 21.5 %gather_fusion = f32[1024,1024]{1,0:T(8,128)} fusion(f32[2,64,12,1024]{3,1,2,0:T(8,128)} %copy.720, s32[1024]{0:T(1024)S(1)} %bitcast.200), kind=kCustom, calls=%fused_computation.2 | custom fusion | bytes 8400896 | tf_op jit(solution)/shard_map/gather | solution.py:134
  276.2 3.3 fusion.35
  293.8 7.2 %add_reduce_fusion.2 = (f32[512]{0:T(512)S(1)}, f32[512]{0:T(512)S(1)}, f32[512,1024]{0,1:T(8,128)S(1)}, f32[512,1024]{0,1:T(8,128)}, f32[512,1024]{0,1:T(8,128)...) fusion(f32[512]{0:T(512)S(1)} %bitcast.208, f32[1,512,1024]{1,2,0:T(8,128)} %copy.713, ...), kind=kLoop, calls=%fused_computation.14 | loop fusion | flops 20970496 | bytes 18884608 | tf_op jit(solution)/shard_map/reduce_sum | solution.py:91
  301.0 3.1 collective-permute-start.8
  306.0 7.2 %collective-permute-start.6 = (f32[1,1]{1,0:T(1,128)}, f32[1,1]{1,0:T(1,128)}, u32[]{:S(2)}, u32[]{:S(2)}) collective-permute-start(f32[1,1]{1,0:T(1,128)} %get-tuple-element.130), channel_id=1, source_target_pairs={{0,1},{1,2},{2,3},{3,4},{4,5},{5,6},{6,7},{7,8},{8,9},{9,10},{10,1... | collective-permute-start | bytes 20 | tf_op jit(solution)/shard_map/ppermute | solution.py:22
  315.2 3.3 collective-permute-done.7
  320.4 78.0 %all-reduce.4 = (f32[]{:T(128)}, f32[]{:T(128)}) all-reduce(f32[]{:T(128)} %get-tuple-element.24, f32[]{:T(128)} %get-tuple-element.23), channel_id=1, replica_groups=mesh['scan'=4,'slab'=64] {'scan','slab'}, use_global_device_ids=true, to_apply=%region_8.10 | all-reduce | flops 2 | bytes 16 | tf_op jit(solution)/shard_map/psum | solution.py:156
  399.7 2.6 collective-permute-start.12
  404.1 5.1 collective-permute-start.10
  411.2 5.5 %add_reduce_fusion = (f32[512]{0:T(512)S(1)}, f32[512]{0:T(512)S(1)}) fusion(f32[512,1024]{0,1:T(8,128)} %get-tuple-element.44, f32[512,1024]{0,1:T(8,128)} %get-tuple-element.43, f32[512,1024]{0,1:T(8,128)} %get-tuple-element.42, f32[512,1024]{0,1:T(8,128)} %get-tuple-element.41, f32[512]{0:T(512)S(1)} %get-tuple-element.35, ...), kind=kLoop, calls=%fused_computation.10 | loop fusion | flops 12581888 | bytes 14690304 | tf_op jit(solution)/shard_map/reduce_sum | solution.py:91
  422.2 5.9 %collective-permute-start.14 = (f32[1,1]{1,0:T(1,128)}, f32[1,1]{1,0:T(1,128)}, u32[]{:S(2)}, u32[]{:S(2)}) collective-permute-start(f32[1,1]{1,0:T(1,128)} %get-tuple-element.120), channel_id=1, source_target_pairs={{0,1},{1,2},{2,3},{3,4},{4,5},{5,6},{6,7},{7,8},{8,9},{9,10},{10,1... | collective-permute-start | bytes 20 | tf_op jit(solution)/shard_map/ppermute | solution.py:22
  430.1 3.3 collective-permute-done.15
  435.3 89.2 %all-reduce.3 = (f32[]{:T(128)}, f32[]{:T(128)}) all-reduce(f32[]{:T(128)} %get-tuple-element.22, f32[]{:T(128)} %get-tuple-element.21), channel_id=1, replica_groups=mesh['scan'=4,'slab'=64] {'scan','slab'}, use_global_device_ids=true, to_apply=%region_14.16 | all-reduce | flops 2 | bytes 16 | tf_op jit(solution)/shard_map/psum | solution.py:156
  525.8 7.8 %add_bitcast_fusion = f32[1,512,1024]{1,2,0:T(8,128)} fusion(f32[512,1024]{0,1:T(8,128)} %get-tuple-element.43, f32[512,1024]{0,1:T(8,128)} %get-tuple-element.40, f32[512,1024]{0,1:T(8,128)} %get-tuple-element.44, f32[512,1024]{0,1:T(8,128)} %get-tuple-element.42, f32[512,1024]{0,1:T(8,128)S(1)} %get-tuple-element.39, f32[512,1024]{0,1:T(8,128)} %get-tuple-element.41, ...), kind=kLoop, calls=%fused_computation.9 | loop fusion | flops 5767168 | bytes 16781312 | tf_op jit(solution)/shard_map/broadcast_in_dim | solution.py:162
  533.7 2.9 copy.721
  (231 shorter events, 54.1 us)
Async XLA Ops:
  0.6 13.3 %copy-start.7 = (s32[3]{0:T(128)S(1)}, s32[3]{0:T(128)}, u32[]{:S(2)}) copy-start(s32[3]{0:T(128)} %constant.79) | copy-start | bytes 40
  0.6 13.4 %copy-start.8 = (s32[3]{0:T(128)S(1)}, s32[3]{0:T(128)}, u32[]{:S(2)}) copy-start(s32[3]{0:T(128)} %constant.82) | copy-start | bytes 40
  0.7 10.2 %copy-start.2 = (s32[1,2,512,1]{2,3,1,0:T(1,128)S(1)}, s32[1,2,512,1]{2,3,1,0:T(1,128)}, u32[]{:S(2)}) copy-start(s32[1,2,512,1]{2,3,1,0:T(1,128)} %param.10) | copy-start | bytes 12292
  0.7 13.5 %copy-start.4 = (s32[1,2,512]{2,1,0:T(2,128)S(1)}, s32[1,2,512]{2,1,0:T(2,128)}, u32[]{:S(2)}) copy-start(s32[1,2,512]{2,1,0:T(2,128)} %param.11) | copy-start | bytes 12292
  3.6 47.5 %collective-permute-start = (f32[512,1024]{0,1:T(8,128)}, f32[512,1024]{0,1:T(8,128)}, u32[]{:S(2)}, u32[]{:S(2)}) collective-permute-start(f32[512,1024]{0,1:T(8,128)} %bitcast.71), channel_id=1, source_target_pairs={{64,0},{128,64},{192,128},{65,1},{129,65},{193,129},{66,2},{130,66... | collective-permute-start | bytes 6291464 | tf_op jit(solution)/shard_map/ppermute | solution.py:34
  4.9 56.3 %collective-permute-start.1 = (f32[512,1024]{0,1:T(8,128)}, f32[512,1024]{0,1:T(8,128)}, u32[]{:S(2)}, u32[]{:S(2)}) collective-permute-start(f32[512,1024]{0,1:T(8,128)} %bitcast.71), channel_id=1, source_target_pairs={{0,64},{64,128},{128,192},{1,65},{65,129},{129,193},{2,66},{66,130... | collective-permute-start | bytes 6291464 | tf_op jit(solution)/shard_map/ppermute | solution.py:34
  91.4 15.3 %copy-start.5 = (s32[1,512]{1,0:T(1,128)S(1)}, s32[1,512]{1,0:T(1,128)}, u32[]{:S(2)}) copy-start(s32[1,512]{1,0:T(1,128)} %param.12) | copy-start | bytes 6148
  91.4 15.4 %copy-start.6 = (f32[4]{0:T(128)S(1)}, f32[4]{0:T(128)}, u32[]{:S(2)}) copy-start(f32[4]{0:T(128)} %param.13) | copy-start | bytes 52
  91.4 15.4 %copy-start.1 = (f32[1,512]{1,0:T(1,128)S(1)}, f32[1,512]{1,0:T(1,128)}, u32[]{:S(2)}) copy-start(f32[1,512]{1,0:T(1,128)} %param.9) | copy-start | bytes 6148
  91.4 154.2 %all-to-all-start.1 = ((f32[2,64,12,1024]{3,0,2,1:T(2,128)}), f32[2,64,12,1024]{3,0,2,1:T(2,128)}, u32[]{:S(2)}, u32[]{:S(2)}) async-start(f32[2,64,12,1024]{3,0,2,1:T(2,128)} %copy.719), calls=%async_computation.1 | async-start | bytes 12582912 | tf_op jit(solution)/shard_map/all_to_all | solution.py:131
  106.9 194.1 %collective-permute-start.4 = (f32[512]{0:T(512)S(1)}, f32[512]{0:T(512)S(1)}, u32[]{:S(2)}, u32[]{:S(2)}) collective-permute-start(f32[512]{0:T(512)S(1)} %get-tuple-element.137), channel_id=1, source_target_pairs={{0,2},{1,3},{2,4},{3,5},{4,6},{5,7},{6,8},{7,9},{8,10},{9,11},{10,... | collective-permute-start | bytes 6152 | tf_op jit(solution)/shard_map/ppermute | solution.py:34
  110.1 190.9 %collective-permute-start.5 = (f32[512]{0:T(512)S(1)}, f32[512]{0:T(512)S(1)}, u32[]{:S(2)}, u32[]{:S(2)}) collective-permute-start(f32[512]{0:T(512)S(1)} %get-tuple-element.137), channel_id=1, source_target_pairs={{2,0},{3,1},{4,2},{5,3},{6,4},{7,5},{8,6},{9,7},{10,8},{11,9},{12,... | collective-permute-start | bytes 6152 | tf_op jit(solution)/shard_map/ppermute | solution.py:34
  112.0 18.7 %collective-permute-start.2 = (f32[1,1]{1,0:T(1,128)}, f32[1,1]{1,0:T(1,128)}, u32[]{:S(2)}, u32[]{:S(2)}) collective-permute-start(f32[1,1]{1,0:T(1,128)} %get-tuple-element.134), channel_id=1, source_target_pairs={{0,1},{1,2},{2,3},{3,4},{4,5},{5,6},{6,7},{7,8},{8,9},{9,10},{10,1... | collective-permute-start | bytes 20 | tf_op jit(solution)/shard_map/ppermute | solution.py:22
  116.9 13.9 %collective-permute-start.3 = (f32[1,1]{1,0:T(1,128)}, f32[1,1]{1,0:T(1,128)}, u32[]{:S(2)}, u32[]{:S(2)}) collective-permute-start(f32[1,1]{1,0:T(1,128)} %get-tuple-element.135), channel_id=1, source_target_pairs={{1,0},{2,1},{3,2},{4,3},{5,4},{6,5},{7,6},{8,7},{9,8},{10,9},{11,1... | collective-permute-start | bytes 20 | tf_op jit(solution)/shard_map/ppermute | solution.py:24
  276.2 3.3 copy-start
  301.0 18.7 %collective-permute-start.8 = (f32[512]{0:T(512)S(1)}, f32[512]{0:T(512)S(1)}, u32[]{:S(2)}, u32[]{:S(2)}) collective-permute-start(f32[512]{0:T(512)S(1)} %get-tuple-element.36), channel_id=1, source_target_pairs={{0,2},{1,3},{2,4},{3,5},{4,6},{5,7},{6,8},{7,9},{8,10},{9,11},{10,... | collective-permute-start | bytes 6152 | tf_op jit(solution)/shard_map/ppermute | solution.py:34
  304.1 15.6 %collective-permute-start.9 = (f32[512]{0:T(512)S(1)}, f32[512]{0:T(512)S(1)}, u32[]{:S(2)}, u32[]{:S(2)}) collective-permute-start(f32[512]{0:T(512)S(1)} %get-tuple-element.36), channel_id=1, source_target_pairs={{2,0},{3,1},{4,2},{5,3},{6,4},{7,5},{8,6},{9,7},{10,8},{11,9},{12,... | collective-permute-start | bytes 6152 | tf_op jit(solution)/shard_map/ppermute | solution.py:34
  306.0 9.1 %collective-permute-start.6 = (f32[1,1]{1,0:T(1,128)}, f32[1,1]{1,0:T(1,128)}, u32[]{:S(2)}, u32[]{:S(2)}) collective-permute-start(f32[1,1]{1,0:T(1,128)} %get-tuple-element.130), channel_id=1, source_target_pairs={{0,1},{1,2},{2,3},{3,4},{4,5},{5,6},{6,7},{7,8},{8,9},{9,10},{10,1... | collective-permute-start | bytes 20 | tf_op jit(solution)/shard_map/ppermute | solution.py:22
  313.2 5.2 collective-permute-start.7
  399.7 18.4 %collective-permute-start.12 = (f32[512]{0:T(512)S(1)}, f32[512]{0:T(512)S(1)}, u32[]{:S(2)}, u32[]{:S(2)}) collective-permute-start(f32[512]{0:T(512)S(1)} %get-tuple-element.34), channel_id=1, source_target_pairs={{0,2},{1,3},{2,4},{3,5},{4,6},{5,7},{6,8},{7,9},{8,10},{9,11},{10,... | collective-permute-start | bytes 6152 | tf_op jit(solution)/shard_map/ppermute | solution.py:34
  402.2 15.8 %collective-permute-start.13 = (f32[512]{0:T(512)S(1)}, f32[512]{0:T(512)S(1)}, u32[]{:S(2)}, u32[]{:S(2)}) collective-permute-start(f32[512]{0:T(512)S(1)} %get-tuple-element.34), channel_id=1, source_target_pairs={{2,0},{3,1},{4,2},{5,3},{6,4},{7,5},{8,6},{9,7},{10,8},{11,9},{12,... | collective-permute-start | bytes 6152 | tf_op jit(solution)/shard_map/ppermute | solution.py:34
  404.1 12.6 %collective-permute-start.10 = (f32[1,1]{1,0:T(1,128)}, f32[1,1]{1,0:T(1,128)}, u32[]{:S(2)}, u32[]{:S(2)}) collective-permute-start(f32[1,1]{1,0:T(1,128)} %get-tuple-element.124), channel_id=1, source_target_pairs={{0,1},{1,2},{2,3},{3,4},{4,5},{5,6},{6,7},{7,8},{8,9},{9,10},{10,1... | collective-permute-start | bytes 20 | tf_op jit(solution)/shard_map/ppermute | solution.py:22
  409.2 7.5 %collective-permute-start.11 = (f32[1,1]{1,0:T(1,128)}, f32[1,1]{1,0:T(1,128)}, u32[]{:S(2)}, u32[]{:S(2)}) collective-permute-start(f32[1,1]{1,0:T(1,128)} %get-tuple-element.125), channel_id=1, source_target_pairs={{1,0},{2,1},{3,2},{4,3},{5,4},{6,5},{7,6},{8,7},{9,8},{10,9},{11,1... | collective-permute-start | bytes 20 | tf_op jit(solution)/shard_map/ppermute | solution.py:24
  418.1 16.6 %collective-permute-start.16 = (f32[512]{0:T(512)S(1)}, f32[512]{0:T(512)S(1)}, u32[]{:S(2)}, u32[]{:S(2)}) collective-permute-start(f32[512]{0:T(512)S(1)} %get-tuple-element.31), channel_id=1, source_target_pairs={{0,2},{1,3},{2,4},{3,5},{4,6},{5,7},{6,8},{7,9},{8,10},{9,11},{10,... | collective-permute-start | bytes 6152 | tf_op jit(solution)/shard_map/ppermute | solution.py:34
  420.3 14.4 %collective-permute-start.17 = (f32[512]{0:T(512)S(1)}, f32[512]{0:T(512)S(1)}, u32[]{:S(2)}, u32[]{:S(2)}) collective-permute-start(f32[512]{0:T(512)S(1)} %get-tuple-element.31), channel_id=1, source_target_pairs={{2,0},{3,1},{4,2},{5,3},{6,4},{7,5},{8,6},{9,7},{10,8},{11,9},{12,... | collective-permute-start | bytes 6152 | tf_op jit(solution)/shard_map/ppermute | solution.py:34
  422.2 7.9 %collective-permute-start.14 = (f32[1,1]{1,0:T(1,128)}, f32[1,1]{1,0:T(1,128)}, u32[]{:S(2)}, u32[]{:S(2)}) collective-permute-start(f32[1,1]{1,0:T(1,128)} %get-tuple-element.120), channel_id=1, source_target_pairs={{0,1},{1,2},{2,3},{3,4},{4,5},{5,6},{6,7},{7,8},{8,9},{9,10},{10,1... | collective-permute-start | bytes 20 | tf_op jit(solution)/shard_map/ppermute | solution.py:22
  428.2 5.2 collective-permute-start.15
  525.8 7.9 %copy-start.3 = (f32[512]{0:T(512)}, f32[512]{0:T(512)S(1)}, u32[]{:S(2)}) copy-start(f32[512]{0:T(512)S(1)} %get-tuple-element.30) | copy-start | bytes 6148
